TPU v7x, 512 devices: a whole 4x4x16 slice. The times are simulated.
512 devices in a mesh: pix: 64 (over z, y), train: 8 (over x, core).
Axes of the slice: x: 4, y: 4, z: 16, core: 2. Of those that a mesh axis runs over, the one named last changes fastest.
Arguments:
- raw_frames: bfloat16 [24, 352, 16384], P('train', None, 'pix'), may hold values from 60 to 160
- gain_section: int32 [24, 352, 16384], P('train', None, 'pix'), may hold values from 0 to 2
- dark_offset: bfloat16 [3, 352, 16384], P(None, None, 'pix'), may hold values from 0 to 40
- rel_gain: float32 [3, 16384], P(None, 'pix'), may hold values from 0.5 to 8
- cycle_label: int32 [16384, 1], P('pix'), may hold values from 0 to 191; in each aligned block of 256 rows (0 to 255, 256 to 511, ...) at most 2 rows name the same one
- cycle_slot: int32 [192], replicated, may hold values from 0 to 191, each once
Outputs:
- two_time: float32 [192, 352, 352], P('pix', 'train')
Inputs may be any that keep to these rules, and one draw needn't show every extreme that they name: `cycle_label`: among the pixels of one index of pix no cycle holds more than 2 pixels; every cycle holds some pixel. `cycle_slot`: A permutation of the cycles.
All inputs are finite; a program needn't handle non-finite values.
Results may differ from a plain program's by a relative error of at most 0.0003.
Values sent between devices are 32-bit elements; how exact they have to be, the bound alone decides.
A program may use at most 64 MiB of HBM per device.

v0:
```python
import jax
import jax.numpy as jnp
from jax import lax
from jax.sharding import PartitionSpec as P

CYCLE_DEV = 3


def on_device(raw_frames, gain_section, dark_offset, rel_gain, cycle_label, cycle_slot):
    trains, pulses, pixels = raw_frames.shape
    owners = lax.axis_size("pix")
    cycle_count = CYCLE_DEV * owners
    slot_depth = 2 * pixels // cycle_count
    section_zero = gain_section == 0
    section_one = gain_section == 1
    offset = jnp.where(
        section_zero, dark_offset[0], jnp.where(section_one, dark_offset[1], dark_offset[2])
    ).astype(jnp.float32)
    factor = jnp.where(section_zero, rel_gain[0], jnp.where(section_one, rel_gain[1], rel_gain[2]))
    intensity = (raw_frames.astype(jnp.float32) - offset) * factor
    pixel_rows = jnp.transpose(intensity, (2, 0, 1)).reshape(pixels, trains * pulses)
    labels = cycle_label[:, 0]
    member = labels[:, None] == jnp.arange(cycle_count, dtype=jnp.int32)[None, :]
    slot_of = jnp.sum(jnp.where(member, cycle_slot[None, :], 0), axis=1)
    running = jnp.cumsum(member.astype(jnp.int32), axis=0)
    within_cycle = jnp.sum(jnp.where(member, running, 0), axis=1) - 1
    cycle_counts = jnp.sum(member.astype(jnp.int32), axis=0)
    slot_member = cycle_slot[:, None] == jnp.arange(cycle_count, dtype=jnp.int32)[None, :]
    slot_counts = jnp.sum(jnp.where(slot_member, cycle_counts[:, None], 0), axis=0)
    position = slot_of * slot_depth + within_cycle
    buffer = (
        jnp.zeros((cycle_count * slot_depth, trains * pulses), jnp.float32)
        .at[position]
        .set(pixel_rows)
    )
    buffer = buffer.reshape(owners, CYCLE_DEV, slot_depth, trains * pulses)
    cycle_tally = slot_counts.astype(jnp.float32).reshape(owners, CYCLE_DEV, 1)
    slot_data = lax.all_to_all(buffer, "pix", split_axis=0, concat_axis=2, tiled=True)
    numbers = lax.all_to_all(cycle_tally, "pix", split_axis=0, concat_axis=2, tiled=True)
    item_count = slot_data.shape[1]
    blocks = slot_data.reshape(item_count, slot_data.shape[2], trains, pulses)
    gram_sum = jnp.einsum("kstf,kstg->kfg", blocks, blocks, precision=lax.Precision.HIGHEST)
    frame_means = jnp.sum(blocks, axis=(1, 2))
    gram_sum, frame_means, number = (
        gram_sum,
        frame_means,
        jnp.sum(numbers.reshape(item_count, numbers.shape[2]), axis=1),
    )
    groups = lax.axis_size("train")
    all_trains = trains * groups
    row_band = pulses // groups
    row_start = lax.axis_index("train") * row_band
    gram_whole, means_whole = lax.psum((gram_sum, frame_means), "train")
    gram_rows = lax.dynamic_slice_in_dim(gram_whole, row_start, row_band, 1)
    means_rows = lax.dynamic_slice_in_dim(means_whole, row_start, row_band, 1)
    cycle_scale = all_trains * number
    return (
        cycle_scale[:, None, None] * gram_rows / (means_rows[:, :, None] * means_whole[:, None, :])
    )


def solution(mesh):
    placed = (
        P("train", None, "pix"),
        P("train", None, "pix"),
        P(None, None, "pix"),
        P(None, "pix"),
        P("pix", None),
        P(),
    )
    return jax.shard_map(
        on_device, mesh=mesh, in_specs=placed, out_specs=P("pix", "train", None), check_vma=False
    )
```

profile of v0, /device:TPU:8, one launch (start us, length us, event | category | flops | bytes accessed | tf_op | source)
XLA Modules:
  0.0 208.9 jit_solution(14207055044721804327)
XLA Ops:
  6.5 0.0 copy-start.1
  6.5 0.0 copy-start
  6.5 0.0 all-reduce.2.cloned.1.call-start
  6.5 0.9 fusion.12
  7.4 0.8 copy.22
  8.2 0.2 fusion.7
  8.5 0.2 copy.23
  8.7 0.9 convert_reduce_fusion
  9.5 0.0 copy-done.1
  9.6 0.0 copy-done
  9.6 0.0 copy-done.2
  9.6 0.4 select_multiply_fusion
  10.0 0.4 copy.24
  10.4 1.9 scatter_custom_fusion
  12.2 1.1 reshape.82
  13.3 104.6 %all_to_all.24 = f32[64,3,2,1056]{3,2,1,0:T(2,128)S(1)} all-to-all(f32[64,3,2,1056]{3,2,1,0:T(2,128)S(1)} %reshape.82), channel_id=1, replica_groups=mesh['pix'=64,'train'=8] {'pix'}, dimensions={0} | all-to-all | bytes 3244032 | tf_op jit(solution)/shard_map/all_to_all | solution.py:38
  117.9 0.6 copy.25
  118.5 3.4 %reshape.83 = f32[3,128,3,352]{3,2,1,0:T(4,128)} reshape(f32[1,3,64,2,1056]{4,3,2,1,0:T(2,128)S(1)} %copy.25) | data formatting | bytes 3244032 | tf_op jit(solution)/shard_map/reshape | solution.py:41
  121.9 6.9 %fusion.2 = f32[3,352,352]{2,1,0:T(8,128)} fusion(f32[3,128,3,352]{3,2,1,0:T(4,128)} %reshape.83), kind=kOutput, calls=%fused_computation.3 | convolution fusion | flops 1712848896 | bytes 3108864 | tf_op jit(solution)/shard_map/kstf,kstg->kfg/dot_general | solution.py:42
  128.7 0.0 all-reduce.2.cloned.1.call-update
  128.8 0.7 copy-done.3
  129.4 0.1 select_reduce_fusion.1
  129.6 0.8 convert_element_type.29
  130.3 6.0 %all-to-all-start = ((f32[64,3,1]{1,2,0:T(1,128)}), f32[64,3,1]{1,2,0:T(1,128)S(1)}, u32[]{:S(2)}, u32[]{:S(2)}) async-start(f32[64,3,1]{1,2,0:T(1,128)} %bitcast.1), calls=%async_computation | async-start | bytes 65536 | tf_op jit(solution)/shard_map/all_to_all | solution.py:39
  136.3 13.7 %all-to-all-done = f32[64,3,1]{1,2,0:T(1,128)S(1)} async-done(((f32[64,3,1]{1,2,0:T(1,128)}), f32[64,3,1]{1,2,0:T(1,128)S(1)}, u32[]{:S(2)}, u32[]{:S(2)}) %all-to-all-start) | async-done | bytes 800 | tf_op jit(solution)/shard_map/all_to_all | solution.py:39
  150.0 0.1 reduce_sum.63
  150.1 0.4 bitcast_reduce_fusion
  150.5 0.1 reduce_sum.67
  150.6 12.8 %psum.15 = f32[3,352]{1,0:T(4,128)S(1)} all-reduce(f32[3,352]{1,0:T(4,128)S(1)} %reduce_sum.68), channel_id=1, replica_groups=mesh['pix'=64,'train'=8] {'train'}, use_global_device_ids=true, to_apply=%region_11.12 | all-reduce | flops 1056 | bytes 8448 | tf_op jit(solution)/shard_map/psum | solution.py:53
  163.5 0.1 constant_dynamic-slice_fusion
  163.5 36.8 %all-reduce.2.cloned.1.call-done = f32[3,352,352]{2,1,0:T(8,128)} async-done(((f32[3,352,352]{2,1,0:T(8,128)}), f32[3,352,352]{2,1,0:T(8,128)}) %all-reduce.2.cloned.1.call-update) | async-done | bytes 1486864 | tf_op jit(solution)/shard_map/psum | solution.py:53
  200.3 1.7 multiply_divide_fusion
  (13 shorter events, 0.2 us)
Async XLA Ops:
  6.5 3.0 %copy-start.1 = (bf16[3,352,256]{2,1,0:T(8,128)(2,1)S(1)}, bf16[3,352,256]{2,1,0:T(8,128)(2,1)}, u32[]{:S(2)}) copy-start(bf16[3,352,256]{2,1,0:T(8,128)(2,1)} %param.8) | copy-start | bytes 1622020
  6.5 3.1 %copy-start = (s32[3,352,256]{2,1,0:T(8,128)S(1)}, s32[3,352,256]{2,1,0:T(8,128)}, u32[]{:S(2)}) copy-start(s32[3,352,256]{2,1,0:T(8,128)} %param.7) | copy-start | bytes 3244036
  6.5 3.1 %copy-start.2 = (bf16[3,352,256]{2,1,0:T(8,128)(2,1)S(1)}, bf16[3,352,256]{2,1,0:T(8,128)(2,1)}, u32[]{:S(2)}) copy-start(bf16[3,352,256]{2,1,0:T(8,128)(2,1)} %param.6) | copy-start | bytes 1622020
  6.5 193.8 %all-reduce.2.cloned.1.call-start = ((), (), s32[]{:S(2)}) async-start(), calls=%async_computation.2 | async-start | bytes 3244032 | tf_op jit(solution)/shard_map/psum | solution.py:53
  128.7 0.7 copy-start.3
  130.3 19.7 %all-to-all-start = ((f32[64,3,1]{1,2,0:T(1,128)}), f32[64,3,1]{1,2,0:T(1,128)S(1)}, u32[]{:S(2)}, u32[]{:S(2)}) async-start(f32[64,3,1]{1,2,0:T(1,128)} %bitcast.1), calls=%async_computation | async-start | bytes 65536 | tf_op jit(solution)/shard_map/all_to_all | solution.py:39
Sparse Core Ops, SparseCore 0:
  128.9 71.4 all-reduce.1
where the time goes:
time: 209 us
  blocking collectives  117 us (56%)
  waiting for transfers between devices  50.5 us (24%)
  between operations  13.5 us (6%)
  local copies, waits for them, and re-layouts  10.7 us (5%)
  matrix products  6.85 us (3%)
  starting transfers between devices  5.95 us (3%)
  other arithmetic  3.88 us (2%)
    all_to_all x1, blocking collectives, on_device(): lax.all_to_all(buffer, 'pix', split_axis=0, concat_axis=2, tiled=True)  105 us
    psum x1, waiting for transfers between devices, on_device(): gram_whole, means_whole = lax.psum((gram_sum, frame_means), 'train')  36.8 us
    all_to_all x1, waiting for transfers between devices, on_device(): lax.all_to_all(cycle_tally, 'pix', split_axis=0, concat_axis=2, tiled=True)  13.7 us
    psum x1, blocking collectives, on_device(): gram_whole, means_whole = lax.psum((gram_sum, frame_means), 'train')  12.8 us
    dot_general x1, matrix products, on_device(): jnp.einsum('kstf,kstg->kfg', blocks, blocks, precision=lax.Precision.HIGH...  6.85 us
    all_to_all x1, starting transfers between devices, on_device(): lax.all_to_all(cycle_tally, 'pix', split_axis=0, concat_axis=2, tiled=True)  5.95 us
  transfers between devices with their start and end apart: 2, of which 2 were waited for; matrix products, arithmetic and copies ran while one was open for 1% of the time, Pallas kernels for 0%

commit v1 on v0

--- a/solution.py
+++ b/solution.py
@@ -35,7 +35,10 @@
     )
     buffer = buffer.reshape(owners, CYCLE_DEV, slot_depth, trains * pulses)
     cycle_tally = slot_counts.astype(jnp.float32).reshape(owners, CYCLE_DEV, 1)
-    slot_data = lax.all_to_all(buffer, "pix", split_axis=0, concat_axis=2, tiled=True)
+    slot_data = jnp.concatenate(
+        lax.all_to_all(jnp.stack(jnp.split(buffer, lax.axis_size("pix"), axis=0)), "pix", 0, 0),
+        axis=2,
+    )
     numbers = lax.all_to_all(cycle_tally, "pix", split_axis=0, concat_axis=2, tiled=True)
     item_count = slot_data.shape[1]
     blocks = slot_data.reshape(item_count, slot_data.shape[2], trains, pulses)

time: 209 us -> 226 us (1.081)
  local copies, waits for them, and re-layouts: 10.7 us -> 25.5 us
    another operation x3 -> x69, local copies, waits for them, and re-layouts: 0.16 us -> 17.2 us  [the longest x65 13.6 us: on_device(): jnp.stack(jnp.split(buffer, lax.axis_size('pix'), axis=0))]
    reshape x2 -> x1, local copies, waits for them, and re-layouts: 4.46 us -> 0.61 us  [on_device(): jnp.concatenate(lax.all_to_all(jnp.stack(jnp.split(buffer, lax.axis_size(...]
where the time goes in v1:
time: 226 us; the launch traced here: 225 us
  blocking collectives  117 us (52%)
  waiting for transfers between devices  51.1 us (23%)
  local copies, waits for them, and re-layouts  25.5 us (11%)
  between operations  14.1 us (6%)
  matrix products  6.86 us (3%)
  starting transfers between devices  5.96 us (3%)
  other arithmetic  3.88 us (2%)
    all_to_all x1, blocking collectives, on_device(): lax.all_to_all(jnp.stack(jnp.split(buffer, lax.axis_size('pix'), axis=0))...  105 us
    psum x1, waiting for transfers between devices, on_device(): gram_whole, means_whole = lax.psum((gram_sum, frame_means), 'train')  37.4 us
    all_to_all x1, waiting for transfers between devices, on_device(): lax.all_to_all(cycle_tally, 'pix', split_axis=0, concat_axis=2, tiled=True)  13.7 us
    another operation x65, local copies, waits for them, and re-layouts, on_device(): jnp.stack(jnp.split(buffer, lax.axis_size('pix'), axis=0))  13.6 us
    psum x1, blocking collectives, on_device(): gram_whole, means_whole = lax.psum((gram_sum, frame_means), 'train')  12.8 us
    dot_general x1, matrix products, on_device(): jnp.einsum('kstf,kstg->kfg', blocks, blocks, precision=lax.Precision.HIGH...  6.86 us
    all_to_all x1, starting transfers between devices, on_device(): lax.all_to_all(cycle_tally, 'pix', split_axis=0, concat_axis=2, tiled=True)  5.96 us
  transfers between devices with their start and end apart: 2, of which 2 were waited for; matrix products, arithmetic and copies ran while one was open for 1% of the time, Pallas kernels for 0%

profile of v1, /device:TPU:8, one launch (start us, length us, event | category | flops | bytes accessed | tf_op | source)
XLA Modules:
  0.0 224.9 jit_solution(13249980173099840045)
XLA Ops:
  6.5 0.9 fusion.16
  7.4 0.8 copy.22
  8.7 0.9 convert_reduce_fusion
  10.4 1.9 scatter_custom_fusion
  12.2 0.7 fusion.15
  12.9 0.7 fusion.14
  13.7 0.7 fusion.13
  14.3 0.8 stack.201
  15.1 0.8 stack.200
  15.9 0.8 stack.199
  16.7 0.8 stack.198
  17.5 0.8 stack.197
  18.3 0.8 stack.196
  19.1 0.8 stack.195
  19.9 0.8 stack.220
  20.7 0.8 stack.219
  21.4 0.8 stack.218
  22.2 0.8 stack.217
  23.0 0.8 stack.216
  23.8 0.8 stack.215
  24.6 0.8 stack.214
  25.4 0.8 stack.213
  26.5 0.8 stack.239
  29.3 104.6 %all_to_all.14 = f32[64,1,3,2,1056]{4,3,2,1,0:T(2,128)S(1)} all-to-all(f32[64,1,3,2,1056]{4,3,2,1,0:T(2,128)S(1)} %constant_dynamic-update-slice_fusion), channel_id=1, replica_groups=mesh['pix'=64,'train'=8] {'pix'}, dimensions={0} | all-to-all | bytes 3244032 | tf_op jit(solution)/shard_map/all_to_all | solution.py:39
  134.5 3.4 %reshape_reshape.3 = f32[3,128,3,352]{3,2,1,0:T(4,128)} reshape(f32[1,3,64,2,1056]{4,3,2,1,0:T(2,128)S(1)} %copy.25) | data formatting | bytes 3244032 | tf_op jit(solution)/shard_map/reshape;reshape | solution.py:44
  137.9 6.9 %fusion.2 = f32[3,352,352]{2,1,0:T(8,128)} fusion(f32[3,128,3,352]{3,2,1,0:T(4,128)} %reshape_reshape.3), kind=kOutput, calls=%fused_computation.3 | convolution fusion | flops 1712848896 | bytes 3108864 | tf_op jit(solution)/shard_map/kstf,kstg->kfg/dot_general | solution.py:45
  144.9 0.8 convert_element_type.29
  145.7 6.0 %all-to-all-start = ((f32[64,3,1]{1,2,0:T(1,128)}), f32[64,3,1]{1,2,0:T(1,128)S(1)}, u32[]{:S(2)}, u32[]{:S(2)}) async-start(f32[64,3,1]{1,2,0:T(1,128)} %bitcast.1), calls=%async_computation | async-start | bytes 65536 | tf_op jit(solution)/shard_map/all_to_all | solution.py:42
  151.7 13.7 %all-to-all-done = f32[64,3,1]{1,2,0:T(1,128)S(1)} async-done(((f32[64,3,1]{1,2,0:T(1,128)}), f32[64,3,1]{1,2,0:T(1,128)S(1)}, u32[]{:S(2)}, u32[]{:S(2)}) %all-to-all-start) | async-done | bytes 800 | tf_op jit(solution)/shard_map/all_to_all | solution.py:42
  166.0 12.8 %psum.15 = f32[3,352]{1,0:T(4,128)S(1)} all-reduce(f32[3,352]{1,0:T(4,128)S(1)} %reduce_sum.68), channel_id=1, replica_groups=mesh['pix'=64,'train'=8] {'train'}, use_global_device_ids=true, to_apply=%region_11.12 | all-reduce | flops 1056 | bytes 8448 | tf_op jit(solution)/shard_map/psum | solution.py:56
  178.9 37.4 %all-reduce.2.cloned.1.call-done = f32[3,352,352]{2,1,0:T(8,128)} async-done(((f32[3,352,352]{2,1,0:T(8,128)}), f32[3,352,352]{2,1,0:T(8,128)}) %all-reduce.2.cloned.1.call-update) | async-done | bytes 1486864 | tf_op jit(solution)/shard_map/psum | solution.py:56
  216.3 1.7 multiply_divide_fusion
  (144 shorter events, 4.5 us)
Async XLA Ops:
  6.5 3.0 %copy-start.1 = (bf16[3,352,256]{2,1,0:T(8,128)(2,1)S(1)}, bf16[3,352,256]{2,1,0:T(8,128)(2,1)}, u32[]{:S(2)}) copy-start(bf16[3,352,256]{2,1,0:T(8,128)(2,1)} %param.8) | copy-start | bytes 1622020
  6.5 3.1 %copy-start = (s32[3,352,256]{2,1,0:T(8,128)S(1)}, s32[3,352,256]{2,1,0:T(8,128)}, u32[]{:S(2)}) copy-start(s32[3,352,256]{2,1,0:T(8,128)} %param.7) | copy-start | bytes 3244036
  6.5 3.1 %copy-start.2 = (bf16[3,352,256]{2,1,0:T(8,128)(2,1)S(1)}, bf16[3,352,256]{2,1,0:T(8,128)(2,1)}, u32[]{:S(2)}) copy-start(bf16[3,352,256]{2,1,0:T(8,128)(2,1)} %param.6) | copy-start | bytes 1622020
  6.5 209.7 %all-reduce.2.cloned.1.call-start = ((), (), s32[]{:S(2)}) async-start(), calls=%async_computation.2 | async-start | bytes 3244032 | tf_op jit(solution)/shard_map/psum | solution.py:56
  137.9 6.9 %copy-start.3 = (s32[192]{0:T(256)S(1)}, s32[192]{0:T(256)}, u32[]{:S(2)}) copy-start(s32[192]{0:T(256)} %param.11) | copy-start | bytes 2308
  145.7 19.7 %all-to-all-start = ((f32[64,3,1]{1,2,0:T(1,128)}), f32[64,3,1]{1,2,0:T(1,128)S(1)}, u32[]{:S(2)}, u32[]{:S(2)}) async-start(f32[64,3,1]{1,2,0:T(1,128)} %bitcast.1), calls=%async_computation | async-start | bytes 65536 | tf_op jit(solution)/shard_map/all_to_all | solution.py:42
Sparse Core Ops, SparseCore 0:
  144.9 71.3 all-reduce.1
